TPU v7x, 32 devices: a whole 2x2x4 slice. The times are simulated.
32 devices in a mesh: vec: 4 (over y, x), walk: 8 (over z, core).
Axes of the slice: x: 2, y: 2, z: 4, core: 2. Of those that a mesh axis runs over, the one named last changes fastest.
Arguments:
- walkers: bfloat16 [128, 1024, 128], P('walk', 'vec'), may hold values from -6 to 6
- inverse: bfloat16 [128, 2, 2, 32, 32], P('walk'), may hold values from -0.75 to 0.75
- vectors: bfloat16 [10240, 1024, 128], P('walk', 'vec'), may hold values from -0.015625 to 0.015625
- sources: int32 [128], replicated, may hold values from 0 to 127
Outputs:
- moved: bfloat16 [128, 1024, 128], P('walk', 'vec')
- force_bias: float32 [2, 128, 10240], P(None, 'vec', 'walk')
Inputs may be any that keep to these rules, and one draw needn't show every extreme that they name: New walker j is a copy of old walker sources[j]; an old walker may be copied many times or not at all.
All inputs are finite; a program needn't handle non-finite values.
Results may differ from a plain program's by a relative error of at most 0.0029.
Values may be sent and summed in bfloat16 or wider, within the bound.
A program may use at most 256 MiB of HBM per device.

v0:
```python
import jax
import jax.numpy as jnp
from jax import lax
from jax.sharding import PartitionSpec as P


def block_of(part):
    real_part, imag_part = (part[:, 0], part[:, 1])
    first = jnp.stack([real_part, imag_part], 3)
    second = jnp.stack([-imag_part, real_part], 3)
    return jnp.stack([first, second], 2)


def green(moved, moved_inverse):
    count, orbitals = (moved.shape[0], moved.shape[1])
    operator = block_of(moved_inverse)
    parts = moved.reshape(count, orbitals, 2, 2, -1)
    theta = jnp.einsum("wpcsk,wsckdi->wpdsi", parts, operator, preferred_element_type=jnp.float32)
    return theta.reshape(count, orbitals, -1).astype(jnp.bfloat16)


def rows_of(theta):
    count, orbitals = (theta.shape[0], theta.shape[1])
    split = theta.reshape(count, orbitals, 2, -1)
    first = jnp.stack([split[:, :, 0], -split[:, :, 1]], 2).reshape(count, -1)
    second = jnp.stack([split[:, :, 1], split[:, :, 0]], 2).reshape(count, -1)
    return jnp.stack([first, second], 0)


def bias_terms(theta, flat_vectors):
    count = theta.shape[0]
    stacked = rows_of(theta).reshape(2 * count, -1)
    product = lax.dot_general(
        stacked, flat_vectors, (((1,), (1,)), ((), ())), preferred_element_type=jnp.float32
    )
    return product.reshape(2, count, flat_vectors.shape[0])


def per_device(walkers, inverse, vectors, sources):
    cycle_index = lax.axis_index("walk")
    local_count = walkers.shape[0]
    flat_vectors = vectors.reshape(vectors.shape[0], -1)
    every_walk, every_inverse = (
        lax.all_gather(walkers, "walk", axis=0, tiled=True),
        lax.all_gather(inverse, "walk", axis=0, tiled=True),
    )
    moved_every = jnp.take(every_walk, sources, axis=0)
    inverse_every = jnp.take(every_inverse, sources, axis=0)
    moved = lax.dynamic_slice_in_dim(moved_every, cycle_index * local_count, local_count)
    theta = green(moved_every, inverse_every)
    partial_bias = bias_terms(theta, flat_vectors)
    force_bias = lax.psum_scatter(partial_bias, "vec", scatter_dimension=1, tiled=True)
    return (moved, force_bias)


def solution(mesh):
    in_specs = (
        P("walk", "vec", None),
        P("walk", None, None, None, None),
        P("walk", "vec", None),
        P(),
    )
    out_specs = (P("walk", "vec", None), P(None, "vec", "walk"))
    return jax.shard_map(
        per_device, mesh=mesh, in_specs=in_specs, out_specs=out_specs, check_vma=False
    )
```

profile of v0, /device:TPU:0, one launch (start us, length us, event | category | flops | bytes accessed | tf_op | source)
XLA Modules:
  0.0 326.8 jit_solution(4765679998027572287)
XLA Ops:
  7.2 0.7 all-gather.5.cloned.1.call-update
  7.9 0.7 all-gather.3.cloned.1.call-update
  8.7 0.0 reduce-scatter.2.cloned.1.call-start
  8.7 121.6 %reshape.53 = bf16[1280,32768,1]{1,0,2:T(8,128)(2,1)} reshape(bf16[1280,256,128]{2,1,0:T(8,128)(2,1)} %param.6) | data formatting | bytes 167772160 | tf_op jit(solution)/shard_map/reshape | solution.py:42
  130.3 5.3 %gather_fusion.1 = bf16[128,2,2,32,32]{4,3,2,1,0:T(8,128)(2,1)} fusion(bf16[128,2,2,32,32]{4,3,2,1,0:T(8,128)(2,1)} %all-gather.5.cloned.1.call-done, s32[1024]{0:T(1024)S(1)} %pad_clamp_fusion), kind=kCustom, calls=%fused_computation.1 | custom fusion | bytes 2097664 | tf_op jit(solution)/shard_map/jit(_take)/gather | solution.py:48
  135.6 6.4 %copy.44 = bf16[128,2,2,32,32]{3,4,2,0,1:T(8,128)(2,1)} copy(bf16[128,2,2,32,32]{4,3,2,1,0:T(8,128)(2,1)} %gather_fusion.1) | data formatting | bytes 2097152 | tf_op jit(solution)/shard_map/jit(_take)/gather | solution.py:48
  142.0 2.6 broadcast_select_fusion
  144.6 0.3 fusion.15
  144.9 1.0 slice_bitcast_fusion
  145.9 3.8 %maximum_bitcast_fusion = (bf16[128,2,1,32,2,32]{3,5,2,4,1,0:T(8,128)(2,1)}, bf16[128,2,1,32,2,32]{3,5,2,4,1,0:T(8,128)(2,1)}) fusion(bf16[128,2,32,1,32]{2,4,3,1,0:T(8,128)(2,1)S(1)} %get-tuple-element.7, bf16[128,2,32,1,32]{2,4,3,1,0:T(8,128)(2,1)S(1)} %get-tuple-element.8, bf16[128,2,32,1,32]{2,4,3,1,0:T(8,128)(2,1)S(1)} %fusion.15), kind=kLoop, calls=%fused_computation.15 | loop fusion | flops 1048576 | bytes 3670016 | tf_op jit(solution)/shard_map/stack | solution.py:11
  149.7 9.9 %gather_fusion = bf16[128,256,128]{2,1,0:T(8,128)(2,1)} fusion(bf16[128,256,128]{2,1,0:T(8,128)(2,1)} %all-gather.3.cloned.1.call-done, s32[1024]{0:T(1024)S(1)} %pad_clamp_fusion), kind=kCustom, calls=%fused_computation | custom fusion | bytes 16777728 | tf_op jit(solution)/shard_map/jit(_take)/gather | solution.py:47
  159.7 11.9 %copy.46 = bf16[128,256,128]{1,2,0:T(8,128)(2,1)} copy(bf16[128,256,128]{2,1,0:T(8,128)(2,1)} %gather_fusion) | data formatting | bytes 16777216 | tf_op jit(solution)/shard_map/jit(_take)/gather | solution.py:47
  171.6 10.9 %fusion.8 = bf16[128,256,2,2,32]{1,4,2,3,0:T(8,128)(2,1)} fusion(bf16[128,2,1,32,2,32]{3,5,2,4,1,0:T(8,128)(2,1)} %get-tuple-element.10, bf16[128,2,1,32,2,32]{3,5,2,4,1,0:T(8,128)(2,1)} %get-tuple-element.9, bf16[128,256,2,2,32]{1,4,3,2,0:T(8,128)(2,1)} %bitcast.31, pred[128]{0:T(512)(128)(4,1)S(1)} %compare_and_fusion), kind=kOutput, calls=%fused_computation.14 | convolution fusion | flops 546308096 | bytes 18874496 | tf_op jit(solution)/shard_map/wpcsk,wsckdi->wpdsi/dot_general | solution.py:18
  182.5 8.1 %copy.48 = bf16[128,256,2,2,32]{1,4,3,2,0:T(8,128)(2,1)} copy(bf16[128,256,2,2,32]{1,4,2,3,0:T(8,128)(2,1)} %fusion.8) | data formatting | bytes 16777216 | tf_op jit(solution)/shard_map/convert_element_type | solution.py:19
  190.6 3.9 %slice_negate_fusion = (bf16[128,256,1,64]{1,3,2,0:T(8,128)(2,1)S(1)}, bf16[128,256,1,64]{1,3,2,0:T(8,128)(2,1)S(1)}, bf16[128,256,1,64]{1,3,2,0:T(8,128)(2,1)S(1)}) fusion(bf16[128,256,2,64]{1,3,2,0:T(8,128)(2,1)} %bitcast.28), kind=kLoop, calls=%fused_computation.27 | loop fusion | flops 2097152 | bytes 20971520 | tf_op jit(solution)/shard_map/neg | solution.py:25
  194.6 6.3 %pad_maximum_fusion = (bf16[128,256,2,64]{1,3,2,0:T(8,128)(2,1)}, bf16[128,256,2,64]{1,3,2,0:T(8,128)(2,1)}) fusion(bf16[128,256,1,64]{1,3,2,0:T(8,128)(2,1)S(1)} %get-tuple-element.2, bf16[128,256,1,64]{1,3,2,0:T(8,128)(2,1)S(1)} %get-tuple-element.4, bf16[128,256,1,64]{1,3,2,0:T(8,128)(2,1)S(1)} %get-tuple-element.3), kind=kLoop, calls=%fused_computation.10 | loop fusion | flops 8388608 | bytes 29360128 | tf_op jit(solution)/shard_map/stack | solution.py:25
  200.8 13.5 %copy.49 = bf16[128,256,2,64]{0,3,2,1:T(8,128)(2,1)} copy(bf16[128,256,2,64]{1,3,2,0:T(8,128)(2,1)} %get-tuple-element.5) | data formatting | bytes 16777216 | tf_op jit(solution)/shard_map/stack | solution.py:25
  214.4 11.9 %copy.51 = bf16[1,128,32768]{2,1,0:T(8,128)(2,1)} copy(bf16[1,128,32768]{1,2,0:T(8,128)(2,1)} %bitcast.29) | data formatting | bytes 16777216 | tf_op jit(solution)/shard_map/stack;reshape | solution.py:27
  226.3 13.5 %copy.50 = bf16[128,256,2,64]{0,3,2,1:T(8,128)(2,1)} copy(bf16[128,256,2,64]{1,3,2,0:T(8,128)(2,1)} %get-tuple-element.6) | data formatting | bytes 16777216 | tf_op jit(solution)/shard_map/stack | solution.py:26
  239.8 11.9 %copy.52 = bf16[1,128,32768]{2,1,0:T(8,128)(2,1)} copy(bf16[1,128,32768]{1,2,0:T(8,128)(2,1)} %bitcast.30) | data formatting | bytes 16777216 | tf_op jit(solution)/shard_map/stack;reshape | solution.py:27
  251.7 35.8 %fusion = f32[2,128,1280]{2,1,0:T(8,128)} fusion(bf16[1280,32768,1]{1,0,2:T(8,128)(2,1)} %reshape.53, bf16[1,128,32768]{2,1,0:T(8,128)(2,1)} %copy.52, bf16[1,128,32768]{2,1,0:T(8,128)(2,1)} %copy.51), kind=kOutput, calls=%fused_computation.2 | convolution fusion | flops 21483225088 | bytes 101974016 | tf_op jit(solution)/shard_map/dot_general | solution.py:33
  287.6 0.1 dynamic-slice
  287.7 2.4 dynamic-slice_select_fusion
  290.0 30.2 %reduce-scatter.2.cloned.1.call-done = f32[2,32,1280]{2,1,0:T(8,128)} async-done(((f32[2,128,1280]{2,1,0:T(8,128)}), f32[2,32,1280]{2,1,0:T(8,128)}) %reduce-scatter.2.cloned.1.call-update) | async-done | bytes 327696 | tf_op jit(solution)/shard_map/reduce_scatter | solution.py:52
  (10 shorter events, 0.1 us)
Async XLA Ops:
  7.2 123.2 %all-gather.5.cloned.1.call-start = ((), (), s32[]{:S(2)}) async-start(), calls=%async_computation.2 | async-start | bytes 4718592 | tf_op jit(solution)/shard_map/all_gather | solution.py:45
  7.9 141.8 %all-gather.3.cloned.1.call-start = ((), (), s32[]{:S(2)}) async-start(), calls=%async_computation.1 | async-start | bytes 9437184 | tf_op jit(solution)/shard_map/all_gather | solution.py:44
  8.6 121.6 %copy-start = (s32[128]{0:T(128)S(1)}, s32[128]{0:T(128)}, u32[]{:S(2)}) copy-start(s32[128]{0:T(128)} %param.7) | copy-start | bytes 1540
  8.7 311.6 %reduce-scatter.2.cloned.1.call-start = ((), (), s32[]{:S(2)}) async-start(), calls=%async_computation.3 | async-start | bytes 1638400 | tf_op jit(solution)/shard_map/reduce_scatter | solution.py:52
Sparse Core Ops, SparseCore 0:
  9.6 49.5 all-gather.4
  60.8 80.8 all-gather.2
  287.7 32.4 reduce-scatter.1
where the time goes:
time: 332 us; the launch traced here: 327 us
  local copies, waits for them, and re-layouts  215 us (65%)
  matrix products  46.7 us (14%)
  waiting for transfers between devices  31.6 us (10%)
  other arithmetic  19.3 us (6%)
  between operations  13.8 us (4%)
    reshape x1, local copies, waits for them, and re-layouts, per_device(): flat_vectors = vectors.reshape(vectors.shape[0], -1)  122 us
    dot_general x1, matrix products, bias_terms(): lax.dot_general(stacked, flat_vectors, (((1,), (1,)), ((), ())), preferre...  35.8 us
    reduce_scatter x1, waiting for transfers between devices, per_device(): lax.psum_scatter(partial_bias, 'vec', scatter_dimension=1, tiled=True)  30.2 us
    another operation x2, local copies, waits for them, and re-layouts, rows_of(): return jnp.stack([first, second], 0)  23.8 us
    gather x2, local copies, waits for them, and re-layouts, per_device(): moved_every = jnp.take(every_walk, sources, axis=0)  21.9 us
    another operation x1, local copies, waits for them, and re-layouts, rows_of(): first = jnp.stack([split[:, :, 0], -split[:, :, 1]], 2).reshape(count, -1)  13.5 us
    another operation x1, local copies, waits for them, and re-layouts, rows_of(): second = jnp.stack([split[:, :, 1], split[:, :, 0]], 2).reshape(count, -1)  13.5 us
    gather x2, local copies, waits for them, and re-layouts, per_device(): inverse_every = jnp.take(every_inverse, sources, axis=0)  11.7 us
  transfers between devices with their start and end apart: 3, of which 1 were waited for; matrix products, arithmetic and copies ran while one was open for 44% of the time, Pallas kernels for 0%

commit v1 on v0

v1 whole, which is shorter than its diff:
```python
import functools

import jax
import jax.numpy as jnp
from jax import lax
from jax.experimental import pallas as pl
from jax.experimental.pallas import tpu as pltpu
from jax.sharding import PartitionSpec as P

VMEM_LIMIT = 66_000_000


def divisor_of(size, choices):
    for choice in choices:
        if size % choice == 0:
            return choice
    return size


def operator_of(packed_inverse):
    plain = packed_inverse.astype(jnp.float32)
    lane = lax.broadcasted_iota(jnp.int32, plain.shape, 1)
    half = plain.shape[1] // 2
    quarter = half // 2
    swapped = jnp.concatenate([-plain[:, half:], plain[:, :half]], 1)
    up = (lane // quarter) % 2 == 0
    theta = jnp.concatenate(
        [
            jnp.where(up, plain, 0.0),
            jnp.where(up, 0.0, plain),
            jnp.where(up, swapped, 0.0),
            jnp.where(up, 0.0, swapped),
        ],
        0,
    )
    first = jnp.concatenate([theta[:, :half], -theta[:, half:]], 1)
    second = jnp.concatenate([theta[:, half:], theta[:, :half]], 1)
    return jnp.concatenate([first, second], 1).astype(jnp.bfloat16)


def theta_kernel(local_count, scalars, *refs):
    walker_refs, inverse_refs = refs[:local_count], refs[local_count : 2 * local_count]
    rows_ref, moved_ref, first_ref, second_ref = refs[2 * local_count :]
    for j in range(local_count):
        operator = operator_of(inverse_refs[j][0])
        both = jnp.dot(walker_refs[j][0], operator, preferred_element_type=jnp.float32)
        both = both.astype(jnp.bfloat16)
        width = both.shape[1] // 2
        first_ref[j] = both[:, :width]
        second_ref[j] = both[:, width:]

    @pl.when(pl.program_id(0) == scalars[0])
    def _():
        for j in range(local_count):
            moved_ref[j] = walker_refs[j][0]

    rows_ref[:, 0] = jnp.swapaxes(first_ref[...], 0, 1)
    rows_ref[:, 1] = jnp.swapaxes(second_ref[...], 0, 1)


def theta_rows(walkers, inverses, inverse_at, scalars, local_count, orbitals, occupied):
    width = walkers.shape[2]
    count = scalars.shape[0] - 1

    def spec(j, height, at):
        return pl.BlockSpec((1, height, width), lambda b, s: (s[1 + b * local_count + j], at, 0))

    each = range(local_count)
    return pl.pallas_call(
        functools.partial(theta_kernel, local_count),
        out_shape=(
            jax.ShapeDtypeStruct((orbitals, 2, count, width), jnp.bfloat16),
            jax.ShapeDtypeStruct((local_count, orbitals, width), jnp.bfloat16),
        ),
        grid_spec=pltpu.PrefetchScalarGridSpec(
            num_scalar_prefetch=1,
            grid=(count // local_count,),
            in_specs=[spec(j, orbitals, 0) for j in each]
            + [spec(j, occupied, inverse_at // occupied) for j in each],
            out_specs=(
                pl.BlockSpec((orbitals, 2, local_count, width), lambda b, s: (0, 0, b, 0)),
                pl.BlockSpec((local_count, orbitals, width), lambda b, s: (0, 0, 0)),
            ),
            scratch_shapes=[pltpu.VMEM((local_count, orbitals, width), jnp.bfloat16)] * 2,
        ),
        cost_estimate=pl.CostEstimate(
            flops=16 * count * orbitals * width * width,
            bytes_accessed=6 * count * orbitals * width,
            transcendentals=0,
        ),
        compiler_params=pltpu.CompilerParams(vmem_limit_bytes=VMEM_LIMIT),
        name="theta_rows",
    )(scalars, *([walkers] * local_count), *([inverses] * local_count))


def bias_kernel(group, rows_ref, vectors_ref, *refs):
    out_ref = refs[-1]
    depth = pl.program_id(1)
    chunk = vectors_ref.shape[1]

    @pl.when(depth == 0)
    def _():
        out_ref[...] = refs[0][...] if len(refs) > 1 else jnp.zeros_like(out_ref)

    for at in range(0, chunk, group):
        turned = jnp.swapaxes(vectors_ref[:, at : at + group, :], 0, 1)
        right = jnp.concatenate([turned[q] for q in range(group)], 1)
        held = rows_ref[pl.ds(depth * chunk + at, group)]
        left = jnp.concatenate([held[q] for q in range(group)], 1)
        out_ref[...] += lax.dot_general(
            left, right, (((1,), (1,)), ((), ())), preferred_element_type=jnp.float32
        )


def bias_terms(rows, vectors, begin, chunk, *before):
    orbitals, height, width = rows.shape
    count = vectors.shape[0]
    tile = divisor_of(count, (256, 128))
    out_spec = pl.BlockSpec((height, tile), lambda g, k: (0, g))
    return pl.pallas_call(
        functools.partial(bias_kernel, divisor_of(chunk, (16,))),
        out_shape=jax.ShapeDtypeStruct((height, count), jnp.float32),
        grid=(count // tile, orbitals // chunk),
        in_specs=[
            pl.BlockSpec((orbitals, height, width), lambda g, k: (0, 0, 0), pipeline_mode=pl.Buffered(1)),
            pl.BlockSpec((tile, chunk, width), lambda g, k: (g, k + begin // chunk, 0)),
        ]
        + [out_spec] * len(before),
        out_specs=out_spec,
        cost_estimate=pl.CostEstimate(
            flops=4 * orbitals * height * width * count,
            bytes_accessed=2 * orbitals * width * (count + height),
            transcendentals=0,
        ),
        compiler_params=pltpu.CompilerParams(vmem_limit_bytes=VMEM_LIMIT),
        name="bias_terms",
    )(rows, vectors, *before)


def per_device(walkers, inverse, vectors, sources):
    local_count, orbitals, width = walkers.shape
    occupied = inverse.shape[-1]
    count = sources.shape[0]
    split = -(-5 * orbitals // (8 * occupied)) * occupied
    small = jnp.transpose(inverse, (0, 3, 1, 2, 4)).reshape(local_count, occupied, width)
    early = jnp.concatenate([walkers[:, :split], small], 1)
    early = lax.all_gather(early, "walk", axis=0, tiled=True)
    late = lax.all_gather(walkers[:, split:], "walk", axis=0, tiled=True)
    scalars = jnp.concatenate([lax.axis_index("walk")[None].astype(jnp.int32), sources])
    rows, moved_early = theta_rows(early, early, split, scalars, local_count, split, occupied)
    bias = bias_terms(rows.reshape(split, 2 * count, width), vectors, 0, occupied)
    rest = orbitals - split
    rows, moved_late = theta_rows(late, early, split, scalars, local_count, rest, occupied)
    bias = bias_terms(rows.reshape(rest, 2 * count, width), vectors, split, occupied, bias)
    moved = jnp.concatenate([moved_early, moved_late], 1)
    force_bias = lax.psum_scatter(
        bias.reshape(2, count, -1), "vec", scatter_dimension=1, tiled=True
    )
    return (moved, force_bias)


def solution(mesh):
    in_specs = (
        P("walk", "vec", None),
        P("walk", None, None, None, None),
        P("walk", "vec", None),
        P(),
    )
    out_specs = (P("walk", "vec", None), P(None, "vec", "walk"))
    return jax.shard_map(
        per_device, mesh=mesh, in_specs=in_specs, out_specs=out_specs, check_vma=False
    )
```

time: 332 us -> 211 us (0.64); the launches traced: 327 us -> 210 us
  local copies, waits for them, and re-layouts: 215 us -> 2.68 us
  Pallas kernels: 0 us -> 97.3 us
  waiting for transfers between devices: 31.6 us -> 92.3 us
  matrix products: 46.7 us -> 0 us
  other arithmetic: 19.3 us -> 3.68 us
    reshape x1, local copies, waits for them, and re-layouts: 122 us -> 0.28 us  [per_device(): jnp.transpose(inverse, (0, 3, 1, 2, 4))]
    pallas_call x0 -> x4, Pallas kernels: none -> 97.3 us  [the longest x2 63.5 us: bias_terms(): pl.pallas_call(functools.partial(bias_kernel, divisor_of(chunk, (16,))),...]
    all_gather x2, waiting for transfers between devices: 0.02 us -> 66 us  [the longest x1 66 us: per_device(): early = lax.all_gather(early, 'walk', axis=0, tiled=True)]
    another operation x5 -> x0, local copies, waits for them, and re-layouts: 51.9 us -> none  [the longest x2 23.8 us: rows_of(): return jnp.stack([first, second], 0)]
    dot_general x2 -> x0, matrix products: 46.7 us -> none  [the longest x1 35.8 us: bias_terms(): lax.dot_general(stacked, flat_vectors, (((1,), (1,)), ((), ())), preferre...]
    gather x4 -> x0, local copies, waits for them, and re-layouts: 33.5 us -> none  [the longest x2 21.9 us: per_device(): moved_every = jnp.take(every_walk, sources, axis=0)]
    another operation x2 -> x0, other arithmetic: 10.1 us -> none  [the longest x1 6.27 us: rows_of(): first = jnp.stack([split[:, :, 0], -split[:, :, 1]], 2).reshape(count, -1)]
    convert_element_type x1 -> x0, local copies, waits for them, and re-layouts: 8.11 us -> none  [green(): return theta.reshape(count, orbitals, -1).astype(jnp.bfloat16)]
  transfers between devices with their start and end apart: 3 -> 3, of which waited for: 1 -> 2; matrix products, arithmetic and copies ran while one was open for 44% -> 2% of each run, Pallas kernels for 0% -> 28%
where the time goes in v1:
time: 211 us; the launch traced here: 210 us
  Pallas kernels  97.3 us (46%)
  waiting for transfers between devices  92.3 us (44%)
  between operations  13.8 us (7%)
  other arithmetic  3.68 us (2%)
  local copies, waits for them, and re-layouts  2.68 us (1%)
    all_gather x1, waiting for transfers between devices, per_device(): early = lax.all_gather(early, 'walk', axis=0, tiled=True)  66 us
    pallas_call x2, Pallas kernels, bias_terms(): pl.pallas_call(functools.partial(bias_kernel, divisor_of(chunk, (16,))),...  63.5 us
    pallas_call x2, Pallas kernels, theta_rows(): pl.pallas_call(functools.partial(theta_kernel, local_count), out_shape=(j...  33.8 us
    reduce_scatter x1, waiting for transfers between devices, per_device(): lax.psum_scatter(bias.reshape(2, count, -1), 'vec', scatter_dimension=1,...  26.2 us
  transfers between devices with their start and end apart: 3, of which 2 were waited for; matrix products, arithmetic and copies ran while one was open for 2% of the time, Pallas kernels for 28%

profile of v1, /device:TPU:0, one launch (start us, length us, event | category | flops | bytes accessed | tf_op | source)
XLA Modules:
  0.0 209.9 jit_solution(1300069763794985289)
XLA Ops:
  7.2 0.0 slice-start
  7.2 0.0 all-gather.3.cloned.1.call-start
  7.2 1.6 copy.7
  8.8 0.0 copy-start
  8.8 0.3 reshape.16
  9.1 0.0 slice-done
  9.1 0.0 copy-start.2
  9.1 1.0 pad_maximum_fusion.1
  10.1 0.0 all-gather.3.cloned.1.call-update
  10.1 0.0 all-gather.5.cloned.1.call-start
  10.2 0.0 copy-done
  10.2 0.8 slice.7
  11.0 0.0 all-gather.5.cloned.1.call-update
  11.0 0.0 reduce-scatter.2.cloned.1.call-start
  11.1 0.6 pad_add_fusion.scalars
  11.7 66.0 %all-gather.3.cloned.1.call-done.refs_0_.refs_1_.refs_2_.refs_3_.refs_4_.refs_5_.refs_6_.refs_7_.refs_8_.refs_9_.refs_10_.refs_11_.refs_12_.refs_13_.refs_14_.refs_15_.refs_16_.refs_17_.refs_18_.refs_19_.refs_20_.refs_21_.refs_22_.refs_23_.refs_24_.refs_25_.refs_26_.refs_27_.refs_28_.refs_29_.refs_30_.refs_31_ = bf16[128,192,128]{2,1,0:T(8,128)(2,1)} async-done(((bf16[16,192,128]{2,1,0:T(8,128)(2,1)}), ...) | async-done | bytes 6291472 | tf_op jit(solution)/shard_map/all_gather | solution.py:147
  77.7 19.2 %theta_rows.2 = (bf16[160,2,128,128]{3,2,1,0:T(8,128)(2,1)}, bf16[16,160,128]{2,1,0:T(8,128)(2,1)}) custom-call(s32[129]{0:T(256)} %pad_add_fusion.scalars, ...), custom_call_target="tpu_custom_call" | custom-call | flops 5368709120 | bytes 15728640 | tf_op jit(solution)/shard_map/theta_rows/pallas_call | solution.py:69
  96.9 39.0 %bias_terms.2.refs_0_ = f32[256,1280]{1,0:T(8,128)} custom-call(bf16[160,256,128]{2,1,0:T(8,128)(2,1)} %bitcast.8, bf16[1280,256,128]{2,1,0:T(8,128)(2,1)} %vectors_ref.3), custom_call_target="tpu_custom_call" | custom-call | flops 26843545600 | bytes 62914560 | tf_op jit(solution)/shard_map/bias_terms/pallas_call | solution.py:120
  135.9 14.7 %theta_rows.3 = (bf16[96,2,128,128]{3,2,1,0:T(8,128)(2,1)}, bf16[16,96,128]{2,1,0:T(8,128)(2,1)}) custom-call(s32[129]{0:T(256)} %pad_add_fusion.scalars, bf16[128,96,128]{2,1,0:T(8,128)(2,1)} %all-gather.5.cloned.1.call-done.refs_0_.refs_1_.refs_2_.refs_3_.refs_4_.refs_5_.refs_6_.refs_7_.refs_8_.refs_9_.refs_10_.refs_11_.refs_12_.refs_13_.refs_14_.refs_15_, ...), custom_call_target="tpu_custom_call" | custom-call | flops 3221225472 | bytes 9437184 | tf_op jit(solution)/shard_map/theta_rows/pallas_call | solution.py:69
  150.6 0.0 copy-start.1
  150.6 24.4 %bias_terms.3 = f32[256,1280]{1,0:T(8,128)} custom-call(bf16[96,256,128]{2,1,0:T(8,128)(2,1)} %bitcast.5, bf16[1280,256,128]{2,1,0:T(8,128)(2,1)} %vectors_ref.3, f32[256,1280]{1,0:T(8,128)} %bias_terms.2.refs_0_), custom_call_target="tpu_custom_call" | custom-call | flops 16106127360 | bytes 37748736 | tf_op jit(solution)/shard_map/bias_terms/pallas_call | solution.py:120
  175.0 0.0 reduce-scatter.2.cloned.1.call-update
  175.0 2.1 pad_maximum_fusion
  177.1 26.2 %reduce-scatter.2.cloned.1.call-done = f32[2,32,1280]{2,1,0:T(8,128)} async-done(((f32[2,128,1280]{2,1,0:T(8,128)}), f32[2,32,1280]{2,1,0:T(8,128)}) %reduce-scatter.2.cloned.1.call-update) | async-done | bytes 327696 | tf_op jit(solution)/shard_map/reduce_scatter | solution.py:156
  (3 shorter events, 0.0 us)
Async XLA Ops:
  7.2 2.0 slice-start
  7.2 70.5 %all-gather.3.cloned.1.call-start = ((), (), s32[]{:S(2)}) async-start(), calls=%async_computation.1 | async-start | bytes 7077888 | tf_op jit(solution)/shard_map/all_gather | solution.py:147
  8.8 1.4 copy-start
  9.1 1.9 copy-start.2
  10.1 125.8 %all-gather.5.cloned.1.call-start = ((), (), s32[]{:S(2)}) async-start(), calls=%async_computation.2 | async-start | bytes 3538944 | tf_op jit(solution)/shard_map/all_gather | solution.py:148
  11.0 192.3 %reduce-scatter.2.cloned.1.call-start = ((), (), s32[]{:S(2)}) async-start(), calls=%async_computation.3 | async-start | bytes 1638400 | tf_op jit(solution)/shard_map/reduce_scatter | solution.py:156
  150.6 24.4 %copy-start.1 = (bf16[16,160,128]{2,1,0:T(8,128)(2,1)S(1)}, bf16[16,160,128]{2,1,0:T(8,128)(2,1)}, u32[]{:S(2)}) copy-start(bf16[16,160,128]{2,1,0:T(8,128)(2,1)} %get-tuple-element.6) | copy-start | bytes 1966084
Sparse Core Ops, SparseCore 0:
  10.3 67.4 all-gather.2
  79.3 36.8 all-gather.4
  175.2 28.1 reduce-scatter.1
